TPU v7x, 32 devices: a whole 2x2x4 slice. The times are simulated.
32 devices in a mesh: row: 8 (over y, x, core), col: 4 (over z).
Axes of the slice: x: 2, y: 2, z: 4, core: 2. Of those that a mesh axis runs over, the one named last changes fastest.
Arguments:
- tiles: bfloat16 [128, 64, 128, 128], P('row', 'col'), may hold values from -0.09375 to 0.09375
- col_index: int32 [128, 64], P('row', 'col'), may hold values from 0 to 15
- counts: int32 [128, 4], P('row', 'col'), may hold values from 1 to 16, as said below
- sketch: bfloat16 [8192, 512], P('col'), may hold values from -6 to 6
Outputs:
- basis: float32 [16384, 512], P(('row', 'col'))
- factor: float32 [512, 512], replicated
Inputs may be any that keep to these rules, and one draw needn't show every extreme that they name: Slots at or beyond counts hold values that are ignored. Some tile row fills all 16 slots of some ignition block.
All inputs are finite; a program needn't handle non-finite values.
Results may differ from a plain program's by a relative error of at most 0.003.
Values may be sent and summed in bfloat16 or wider, within the bound.
No kernel may reach another device: no remote copies, remote signals or barrier semaphores. Data moves between devices by JAX's collectives and lax.ppermute only.
A program may use at most 128 MiB of HBM per device.

v0:
```python
import jax
import jax.numpy as jnp
from jax import lax
from jax.sharding import PartitionSpec as P


def swapped(value, axis, distance):
    mask = 2**distance
    pairs = [(source, source ^ mask) for source in range(lax.axis_size(axis))]
    return lax.ppermute(value, axis, pairs)


def local(tiles, col_index, counts, sketch):
    tile_rows, slots, tile = (tiles.shape[0], tiles.shape[1], tiles.shape[2])
    width = sketch.shape[1]
    col_tiles = sketch.shape[0] // tile
    total_rows = tile_rows * tile * lax.axis_size("row")
    live = (jnp.arange(slots)[None, :] < counts).astype(jnp.bfloat16)
    live_float = live.astype(jnp.float32)
    share_rows = tile_rows * tile // lax.axis_size("col")

    def project_rows(x_tiles):
        many = share_rows * lax.axis_size("col") // tile
        picked = jnp.take(x_tiles, col_index, axis=0) * live[:, :, None, None]
        matrix_product = jnp.einsum(
            "rsab,rsbk->rak", tiles, picked, preferred_element_type=jnp.float32
        )
        return lax.psum_scatter(
            matrix_product.reshape(many * tile, width), "col", scatter_dimension=0, tiled=True
        )

    def orthonormal(panel):
        gram = jnp.dot(
            panel.T, panel, precision=lax.Precision.HIGHEST, preferred_element_type=jnp.float32
        )
        for level in range(lax.axis_size(("row", "col")).bit_length() - 1):
            gram = gram + swapped(gram, ("row", "col"), level)
        lower = jnp.linalg.cholesky(gram / total_rows)
        basis = lax.linalg.triangular_solve(
            lower, panel, left_side=False, lower=True, transpose_a=True
        )
        return (basis, lower.T)

    first = project_rows(sketch.reshape(col_tiles, tile, width))
    first_q, unused = orthonormal(first)
    q_local = lax.all_gather(first_q.astype(jnp.bfloat16), "col", axis=0, tiled=True).reshape(
        tile_rows, tile, width
    )

    def accumulate(index, total):
        matrix_product = jnp.einsum(
            "sab,ak->sbk", tiles[index], q_local[index], preferred_element_type=jnp.float32
        )
        matrix_product = matrix_product * live_float[index][:, None, None]
        return total.at[col_index[index]].add(matrix_product)

    back_part = lax.fori_loop(
        0, tile_rows, accumulate, jnp.zeros((col_tiles, tile, width), jnp.float32)
    )
    back = lax.psum(back_part, "row").astype(jnp.bfloat16)
    second = project_rows(back)
    basis, factor = orthonormal(second)
    return (basis, factor)


def solution(mesh):
    return jax.shard_map(
        local,
        mesh=mesh,
        in_specs=(P("row", "col", None, None), P("row", "col"), P("row", "col"), P("col", None)),
        out_specs=(P(("row", "col"), None), P()),
        check_vma=False,
    )
```

profile of v0, /device:TPU:0, one launch (start us, length us, event | category | flops | bytes accessed | tf_op | source)
XLA Modules:
  0.0 1161.6 jit_solution(8305503465037512460)
XLA Ops:
  8.9 13.8 %gather_fusion = bf16[256,128,512]{2,1,0:T(8,128)(2,1)} fusion(bf16[16,128,512]{2,1,0:T(8,128)(2,1)S(1)} %bitcast.151, s32[1024]{0:T(1024)S(1)} %pad_clamp_fusion), kind=kCustom, calls=%fused_computation.clone | custom fusion | bytes 67109888 | tf_op jit(solution)/shard_map/jit(_take)/gather | solution.py:24
  22.7 19.1 %fusion.9 = f32[16,512,128,1]{1,2,3,0:T(8,128)} fusion(bf16[16,16,128,128]{3,2,1,0:T(8,128)(2,1)} %param.11, bf16[16,16,128,512]{3,2,1,0:T(8,128)(2,1)} %bitcast.153, pred[16,16]{1,0:T(8,128)(4,1)S(1)} %get-tuple-element.199, bf16[16,16]{1,0:T(8,128)(2,1)S(1)} %get-tuple-element.194), kind=kOutput, calls=%fused_computation.22 | convolution fusion | flops 4378853376 | bytes 46138112 | tf_op jit(solution)/shard_map/rsab,rsbk->rak/dot_general | solution.py:25
  42.0 79.5 %reduce-scatter.3.cloned.1.call-done = f32[512,512]{1,0:T(8,128)} async-done(((f32[2048,512]{1,0:T(8,128)}), f32[512,512]{1,0:T(8,128)}) %reduce-scatter.3.cloned.1.call-update) | async-done | bytes 1048592 | tf_op jit(solution)/shard_map/reduce_scatter | solution.py:28
  126.5 23.1 %collective-permute-done = f32[512,512]{0,1:T(8,128)S(1)} collective-permute-done((f32[512,512]{0,1:T(8,128)S(1)}, f32[512,512]{0,1:T(8,128)S(1)}, u32[]{:S(2)}, u32[]{:S(2)}) %collective-permute-start) | collective-permute-done | bytes 1048608 | tf_op jit(solution)/shard_map/ppermute | solution.py:10
  153.1 44.7 %collective-permute-done.1 = f32[512,512]{0,1:T(8,128)S(1)} collective-permute-done((f32[512,512]{0,1:T(8,128)S(1)}, f32[512,512]{0,1:T(8,128)S(1)}, u32[]{:S(2)}, u32[]{:S(2)}) %collective-permute-start.1) | collective-permute-done | bytes 1048608 | tf_op jit(solution)/shard_map/ppermute | solution.py:10
  202.5 23.7 %collective-permute-done.3 = f32[512,512]{0,1:T(8,128)S(1)} collective-permute-done((f32[512,512]{0,1:T(8,128)S(1)}, f32[512,512]{0,1:T(8,128)S(1)}, u32[]{:S(2)}, u32[]{:S(2)}) %collective-permute-start.3) | collective-permute-done | bytes 1048608 | tf_op jit(solution)/shard_map/ppermute | solution.py:10
  227.9 23.0 %collective-permute-done.4 = f32[512,512]{0,1:T(8,128)} collective-permute-done((f32[512,512]{0,1:T(8,128)S(1)}, f32[512,512]{0,1:T(8,128)}, u32[]{:S(2)}, u32[]{:S(2)}) %collective-permute-start.4) | collective-permute-done | bytes 1048608 | tf_op jit(solution)/shard_map/ppermute | solution.py:10
  254.0 11.7 %cholesky.286 = f32[128,128]{1,0:T(8,128)S(1)} custom-call(f32[128,128]{1,0:T(8,128)S(1)} %cholesky.426), custom_call_target="Cholesky" | custom-call | tf_op jit(solution)/shard_map/jit(cholesky)/cholesky | solution.py:38
  278.2 12.1 %cholesky.305 = f32[128,128]{1,0:T(8,128)S(1)} custom-call(f32[128,128]{1,0:T(8,128)S(1)} %cholesky.430), custom_call_target="Cholesky" | custom-call | tf_op jit(solution)/shard_map/jit(cholesky)/cholesky | solution.py:38
  326.7 11.9 %cholesky.343 = f32[128,128]{1,0:T(8,128)S(1)} custom-call(f32[128,128]{1,0:T(8,128)S(1)} %convolution_subtract_fusion.11), custom_call_target="Cholesky" | custom-call | tf_op jit(solution)/shard_map/jit(cholesky)/cholesky | solution.py:38
  350.5 39.3 %custom-call.30 = f32[4,128,128]{1,2,0:T(8,128)S(1)} custom-call(f32[4,128,128]{2,1,0:T(8,128)S(1)} %get-tuple-element.129), custom_call_target="InvertDiagBlocksLowerTriangular" | custom-call | tf_op jit(solution)/shard_map/triangular_solve/custom-call.3 | solution.py:39
  395.5 45.8 %all-gather.2.cloned.1.call-done = bf16[2048,512]{0,1:T(8,128)(2,1)} async-done(((bf16[512,512]{0,1:T(8,128)(2,1)}), bf16[2048,512]{0,1:T(8,128)(2,1)}) %all-gather.2.cloned.1.call-update) | async-done | bytes 2097168 | tf_op jit(solution)/shard_map/all_gather | solution.py:46
  446.7 221.1 %while.17 = (s32[]{:T(128)}, f32[16,128,512]{2,1,0:T(8,128)}, s32[16,16]{1,0:T(8,128)}, bf16[16,16,128,128]{3,2,1,0:T(8,128)(2,1)}, bf16[16,128,512]{2,1,0:T(8,128)(2,1)S(1)}, /*index=5*/f32[16,16]{1,0:T(8,128)S(1)}, s32[]{:T(128)}) while((s32[]{:T(128)}, f32[16,128,512]{2,1,0:T(8,128)}, s32[16,16]{1,0:T(8,128)}, ...), condition=%wide.region_11.15_spmd, body=%wide.region_9.14_spmd.sunk | while | flops 270532672 | bytes 17434516 | solution.py:57
  667.8 88.4 %all-reduce.2 = bf16[16,128,512]{2,1,0:T(8,128)(2,1)S(1)} all-reduce(f32[16,128,512]{2,1,0:T(8,128)} %get-tuple-element.114), channel_id=1, replica_groups=mesh['row'=8,'col'=4] {'row'}, use_global_device_ids=true, to_apply=%region_12.16 | all-reduce | flops 1048576 | bytes 6291456 | tf_op jit(solution)/shard_map/psum | solution.py:60
  756.2 13.8 %gather_fusion.1 = bf16[256,128,512]{2,1,0:T(8,128)(2,1)} fusion(bf16[16,128,512]{2,1,0:T(8,128)(2,1)S(1)} %all-reduce.2, s32[1024]{0:T(1024)S(1)} %pad_clamp_fusion), kind=kCustom, calls=%fused_computation.1.clone | custom fusion | bytes 67109888 | tf_op jit(solution)/shard_map/jit(_take)/gather | solution.py:24
  770.0 19.4 %fusion.8 = f32[16,512,128,1]{1,2,3,0:T(8,128)} fusion(bf16[16,16,128,128]{3,2,1,0:T(8,128)(2,1)} %get-tuple-element.379, bf16[16,16,128,512]{3,2,1,0:T(8,128)(2,1)} %bitcast.152, pred[16,16]{1,0:T(8,128)(4,1)S(1)} %get-tuple-element.199, bf16[16,16]{1,0:T(8,128)(2,1)S(1)} %get-tuple-element.194), kind=kOutput, calls=%fused_computation.20 | convolution fusion | flops 4378853376 | bytes 46138112 | tf_op jit(solution)/shard_map/rsab,rsbk->rak/dot_general | solution.py:25
  789.5 75.0 %reduce-scatter.5.cloned.1.call-done = f32[512,512]{1,0:T(8,128)} async-done(((f32[2048,512]{1,0:T(8,128)}), f32[512,512]{1,0:T(8,128)}) %reduce-scatter.5.cloned.1.call-update) | async-done | bytes 1048592 | tf_op jit(solution)/shard_map/reduce_scatter | solution.py:28
  869.5 23.1 %collective-permute-done.5 = f32[512,512]{0,1:T(8,128)S(1)} collective-permute-done((f32[512,512]{0,1:T(8,128)S(1)}, f32[512,512]{0,1:T(8,128)S(1)}, u32[]{:S(2)}, u32[]{:S(2)}) %collective-permute-start.5) | collective-permute-done | bytes 1048608 | tf_op jit(solution)/shard_map/ppermute | solution.py:10
  896.1 44.7 %collective-permute-done.6 = f32[512,512]{0,1:T(8,128)S(1)} collective-permute-done((f32[512,512]{0,1:T(8,128)S(1)}, f32[512,512]{0,1:T(8,128)S(1)}, u32[]{:S(2)}, u32[]{:S(2)}) %collective-permute-start.6) | collective-permute-done | bytes 1048608 | tf_op jit(solution)/shard_map/ppermute | solution.py:10
  945.5 23.7 %collective-permute-done.8 = f32[512,512]{0,1:T(8,128)S(1)} collective-permute-done((f32[512,512]{0,1:T(8,128)S(1)}, f32[512,512]{0,1:T(8,128)S(1)}, u32[]{:S(2)}, u32[]{:S(2)}) %collective-permute-start.8) | collective-permute-done | bytes 1048608 | tf_op jit(solution)/shard_map/ppermute | solution.py:10
  971.0 22.9 %collective-permute-done.9 = f32[512,512]{0,1:T(8,128)S(1)} collective-permute-done((f32[512,512]{0,1:T(8,128)S(1)}, f32[512,512]{0,1:T(8,128)S(1)}, u32[]{:S(2)}, u32[]{:S(2)}) %collective-permute-start.9) | collective-permute-done | bytes 1048608 | tf_op jit(solution)/shard_map/ppermute | solution.py:10
  1021.4 11.9 %cholesky.377 = f32[128,128]{1,0:T(8,128)S(1)} custom-call(f32[128,128]{1,0:T(8,128)S(1)} %cholesky.443), custom_call_target="Cholesky" | custom-call | tf_op jit(solution)/shard_map/jit(cholesky)/cholesky | solution.py:38
  1072.6 11.9 %cholesky.415 = f32[128,128]{1,0:T(8,128)S(1)} custom-call(f32[128,128]{1,0:T(8,128)S(1)} %convolution_subtract_fusion.10), custom_call_target="Cholesky" | custom-call | tf_op jit(solution)/shard_map/jit(cholesky)/cholesky | solution.py:38
  1103.3 40.1 %custom-call.34 = f32[4,128,128]{1,2,0:T(8,128)S(1)} custom-call(f32[4,128,128]{2,1,0:T(8,128)} %copy-done.6), custom_call_target="InvertDiagBlocksLowerTriangular" | custom-call | tf_op jit(solution)/shard_map/triangular_solve/custom-call.3 | solution.py:39
  (213 shorter events, 439.1 us)
Async XLA Ops:
  7.2 1.8 copy-start
  7.2 114.3 %reduce-scatter.3.cloned.1.call-start = ((), (), s32[]{:S(2)}) async-start(), calls=%async_computation.2 | async-start | bytes 5242880 | tf_op jit(solution)/shard_map/reduce_scatter | solution.py:28
  41.8 399.5 %all-gather.2.cloned.1.call-start = ((), (), s32[]{:S(2)}) async-start(), calls=%async_computation.3 | async-start | bytes 2621440 | tf_op jit(solution)/shard_map/all_gather | solution.py:46
  124.9 24.7 %collective-permute-start = (f32[512,512]{0,1:T(8,128)S(1)}, f32[512,512]{0,1:T(8,128)S(1)}, u32[]{:S(2)}, u32[]{:S(2)}) collective-permute-start(f32[512,512]{0,1:T(8,128)S(1)} %fusion.93), channel_id=1, source_target_pairs={{0,1},{1,0},{2,3},{3,2},{4,5},{5,4},{6,7},{7,6},{8,9},{9,8},{10,11... | collective-permute-start | bytes 3145736 | tf_op jit(solution)/shard_map/ppermute | solution.py:10
  149.8 48.0 %collective-permute-start.1 = (f32[512,512]{0,1:T(8,128)S(1)}, f32[512,512]{0,1:T(8,128)S(1)}, u32[]{:S(2)}, u32[]{:S(2)}) collective-permute-start(f32[512,512]{0,1:T(8,128)S(1)} %add.113), channel_id=1, source_target_pairs={{0,2},{1,3},{2,0},{3,1},{4,6},{5,7},{6,4},{7,5},{8,10},{9,11},{10,... | collective-permute-start | bytes 3145736 | tf_op jit(solution)/shard_map/ppermute | solution.py:10
  198.0 2.7 collective-permute-start.2
  200.9 25.3 %collective-permute-start.3 = (f32[512,512]{0,1:T(8,128)S(1)}, f32[512,512]{0,1:T(8,128)S(1)}, u32[]{:S(2)}, u32[]{:S(2)}) collective-permute-start(f32[512,512]{0,1:T(8,128)S(1)} %add.115), channel_id=1, source_target_pairs={{0,8},{1,9},{2,10},{3,11},{4,12},{5,13},{6,14},{7,15},{8,0},{9,1},... | collective-permute-start | bytes 3145736 | tf_op jit(solution)/shard_map/ppermute | solution.py:10
  226.4 163.4 %copy-start.2 = (f32[512,512]{1,0:T(8,128)S(1)}, f32[512,512]{1,0:T(8,128)}, u32[]{:S(2)}) copy-start(f32[512,512]{1,0:T(8,128)} %reduce-scatter.3.cloned.1.call-done) | copy-start | bytes 3145732
  226.4 24.5 %collective-permute-start.4 = (f32[512,512]{0,1:T(8,128)S(1)}, f32[512,512]{0,1:T(8,128)}, u32[]{:S(2)}, u32[]{:S(2)}) collective-permute-start(f32[512,512]{0,1:T(8,128)S(1)} %add.116), channel_id=1, source_target_pairs={{0,16},{1,17},{2,18},{3,19},{4,20},{5,21},{6,22},{7,23},{8,24},{9,... | collective-permute-start | bytes 3145736 | tf_op jit(solution)/shard_map/ppermute | solution.py:10
  253.0 1.0 copy-start.4
  395.5 469.1 %reduce-scatter.5.cloned.1.call-start = ((), (), s32[]{:S(2)}) async-start(), calls=%async_computation.4 | async-start | bytes 5242880 | tf_op jit(solution)/shard_map/reduce_scatter | solution.py:28
  868.0 24.7 %collective-permute-start.5 = (f32[512,512]{0,1:T(8,128)S(1)}, f32[512,512]{0,1:T(8,128)S(1)}, u32[]{:S(2)}, u32[]{:S(2)}) collective-permute-start(f32[512,512]{0,1:T(8,128)S(1)} %fusion.94), channel_id=1, source_target_pairs={{0,1},{1,0},{2,3},{3,2},{4,5},{5,4},{6,7},{7,6},{8,9},{9,8},{10,11... | collective-permute-start | bytes 3145736 | tf_op jit(solution)/shard_map/ppermute | solution.py:10
  892.8 47.9 %collective-permute-start.6 = (f32[512,512]{0,1:T(8,128)S(1)}, f32[512,512]{0,1:T(8,128)S(1)}, u32[]{:S(2)}, u32[]{:S(2)}) collective-permute-start(f32[512,512]{0,1:T(8,128)S(1)} %add.118), channel_id=1, source_target_pairs={{0,2},{1,3},{2,0},{3,1},{4,6},{5,7},{6,4},{7,5},{8,10},{9,11},{10,... | collective-permute-start | bytes 3145736 | tf_op jit(solution)/shard_map/ppermute | solution.py:10
  941.0 2.7 collective-permute-start.7
  943.9 25.3 %collective-permute-start.8 = (f32[512,512]{0,1:T(8,128)S(1)}, f32[512,512]{0,1:T(8,128)S(1)}, u32[]{:S(2)}, u32[]{:S(2)}) collective-permute-start(f32[512,512]{0,1:T(8,128)S(1)} %add.120), channel_id=1, source_target_pairs={{0,8},{1,9},{2,10},{3,11},{4,12},{5,13},{6,14},{7,15},{8,0},{9,1},... | collective-permute-start | bytes 3145736 | tf_op jit(solution)/shard_map/ppermute | solution.py:10
  969.4 174.0 %copy-start.3 = (f32[512,512]{1,0:T(8,128)S(1)}, f32[512,512]{1,0:T(8,128)}, u32[]{:S(2)}) copy-start(f32[512,512]{1,0:T(8,128)} %reduce-scatter.5.cloned.1.call-done) | copy-start | bytes 3145732
  969.4 24.4 %collective-permute-start.9 = (f32[512,512]{0,1:T(8,128)S(1)}, f32[512,512]{0,1:T(8,128)S(1)}, u32[]{:S(2)}, u32[]{:S(2)}) collective-permute-start(f32[512,512]{0,1:T(8,128)S(1)} %add.121), channel_id=1, source_target_pairs={{0,16},{1,17},{2,18},{3,19},{4,20},{5,21},{6,22},{7,23},{8,24},{9,... | collective-permute-start | bytes 3145736 | tf_op jit(solution)/shard_map/ppermute | solution.py:10
  994.6 1.0 copy-start.5
  1070.3 84.5 %copy-start.1 = (bf16[2048,512]{1,0:T(8,128)(2,1)S(1)}, bf16[2048,512]{1,0:T(8,128)(2,1)}, u32[]{:S(2)}) copy-start(bf16[2048,512]{1,0:T(8,128)(2,1)} %param.14) | copy-start | bytes 6291460
  1102.6 0.7 copy-start.6
Sparse Core Ops, SparseCore 0:
  41.9 79.5 reduce-scatter.2
  395.6 45.7 all-gather.1
  789.6 74.8 reduce-scatter.4
where the time goes:
time: 1170 us; the launch traced here: 1160 us
  waiting for transfers between devices  435 us (37%)
  other arithmetic  411 us (35%)
  matrix products  130 us (11%)
  blocking collectives  88.4 us (8%)
  local copies, waits for them, and re-layouts  61.3 us (5%)
  between operations  19.6 us (2%)
  starting transfers between devices  16.2 us (1%)
    ppermute x10, waiting for transfers between devices, swapped(): return lax.ppermute(value, axis, pairs)  234 us
    another operation x30, other arithmetic, orthonormal(): lower = jnp.linalg.cholesky(gram / total_rows)  161 us
    reduce_scatter x2, waiting for transfers between devices, project_rows(): lax.psum_scatter(matrix_product.reshape(many * tile, width), 'col', scatt...  155 us
    scatter-add x16, other arithmetic, accumulate(): return total.at[col_index[index]].add(matrix_product)  151 us
    psum x1, blocking collectives, local(): back = lax.psum(back_part, 'row').astype(jnp.bfloat16)  88.4 us
    another operation x5, other arithmetic, orthonormal(): lax.linalg.triangular_solve(lower, panel, left_side=False, lower=True, tr...  79.6 us
    dot_general x16, matrix products, accumulate(): jnp.einsum('sab,ak->sbk', tiles[index], q_local[index], preferred_element...  59.4 us
    all_gather x1, waiting for transfers between devices, local(): lax.all_gather(first_q.astype(jnp.bfloat16), 'col', axis=0, tiled=True)  45.8 us
  transfers between devices with their start and end apart: 13, of which 13 were waited for; matrix products, arithmetic and copies ran while one was open for 0% of the time, Pallas kernels for 0%

commit v1 on v0

--- a/solution.py
+++ b/solution.py
@@ -2,6 +2,12 @@
 import jax.numpy as jnp
 from jax import lax
 from jax.sharding import PartitionSpec as P
+
+
+def gather_and_add(x, mesh_axis):
+    parts = lax.all_gather(x, mesh_axis, axis=0, tiled=False)
+    total = parts.sum(axis=0)
+    return total
 
 
 def swapped(value, axis, distance):
@@ -57,7 +63,7 @@
     back_part = lax.fori_loop(
         0, tile_rows, accumulate, jnp.zeros((col_tiles, tile, width), jnp.float32)
     )
-    back = lax.psum(back_part, "row").astype(jnp.bfloat16)
+    back = gather_and_add(back_part, "row").astype(jnp.bfloat16)
     second = project_rows(back)
     basis, factor = orthonormal(second)
     return (basis, factor)

time: 1170 us -> 1260 us (1.077)
  waiting for transfers between devices: 435 us -> 598 us
  blocking collectives: 88.4 us -> 0 us
  other arithmetic: 411 us -> 424 us
    all_gather x0 -> x1, waiting for transfers between devices: none -> 161 us  [gather_and_add(): parts = lax.all_gather(x, mesh_axis, axis=0, tiled=False)]
    psum x1 -> x0, blocking collectives: 88.4 us -> none  [local(): back = lax.psum(back_part, 'row').astype(jnp.bfloat16)]
    reduce_sum x0 -> x1, other arithmetic: none -> 13.3 us  [gather_and_add(): total = parts.sum(axis=0)]
  transfers between devices with their start and end apart: 13 -> 14, of which waited for: 13 -> 14; matrix products, arithmetic and copies ran while one was open for 0% -> 0% of each run, Pallas kernels for 0% -> 0%
where the time goes in v1:
time: 1260 us; the launch traced here: 1250 us
  waiting for transfers between devices  598 us (47%)
  other arithmetic  424 us (34%)
  matrix products  130 us (10%)
  local copies, waits for them, and re-layouts  61.5 us (5%)
  between operations  19.6 us (2%)
  starting transfers between devices  16.2 us (1%)
    ppermute x10, waiting for transfers between devices, swapped(): return lax.ppermute(value, axis, pairs)  234 us
    all_gather x1, waiting for transfers between devices, gather_and_add(): parts = lax.all_gather(x, mesh_axis, axis=0, tiled=False)  161 us
    another operation x30, other arithmetic, orthonormal(): lower = jnp.linalg.cholesky(gram / total_rows)  161 us
    reduce_scatter x2, waiting for transfers between devices, project_rows(): lax.psum_scatter(matrix_product.reshape(many * tile, width), 'col', scatt...  156 us
    scatter-add x16, other arithmetic, accumulate(): return total.at[col_index[index]].add(matrix_product)  150 us
    another operation x5, other arithmetic, orthonormal(): lax.linalg.triangular_solve(lower, panel, left_side=False, lower=True, tr...  79.6 us
    dot_general x16, matrix products, accumulate(): jnp.einsum('sab,ak->sbk', tiles[index], q_local[index], preferred_element...  59.4 us
    all_gather x1, waiting for transfers between devices, local(): lax.all_gather(first_q.astype(jnp.bfloat16), 'col', axis=0, tiled=True)  45.8 us
  transfers between devices with their start and end apart: 14, of which 14 were waited for; matrix products, arithmetic and copies ran while one was open for 0% of the time, Pallas kernels for 0%

profile of v1, /device:TPU:0, one launch (start us, length us, event | category | flops | bytes accessed | tf_op | source)
XLA Modules:
  0.0 1249.6 jit_solution(14433400481700179065)
XLA Ops:
  8.9 13.8 %gather_fusion = bf16[256,128,512]{2,1,0:T(8,128)(2,1)} fusion(bf16[16,128,512]{2,1,0:T(8,128)(2,1)S(1)} %bitcast.152, s32[1024]{0:T(1024)S(1)} %pad_clamp_fusion), kind=kCustom, calls=%fused_computation.clone | custom fusion | bytes 67109888 | tf_op jit(solution)/shard_map/jit(_take)/gather | solution.py:30
  22.8 19.1 %fusion.9 = f32[16,512,128,1]{1,2,3,0:T(8,128)} fusion(bf16[16,16,128,128]{3,2,1,0:T(8,128)(2,1)} %param.11, bf16[16,16,128,512]{3,2,1,0:T(8,128)(2,1)} %bitcast.155, pred[16,16]{1,0:T(8,128)(4,1)S(1)} %get-tuple-element.207, bf16[16,16]{1,0:T(8,128)(2,1)S(1)} %get-tuple-element.202), kind=kOutput, calls=%fused_computation.22 | convolution fusion | flops 4378853376 | bytes 46138112 | tf_op jit(solution)/shard_map/rsab,rsbk->rak/dot_general | solution.py:31
  42.1 79.5 %reduce-scatter.3.cloned.1.call-done = f32[512,512]{1,0:T(8,128)} async-done(((f32[2048,512]{1,0:T(8,128)}), f32[512,512]{1,0:T(8,128)}) %reduce-scatter.3.cloned.1.call-update) | async-done | bytes 1048592 | tf_op jit(solution)/shard_map/reduce_scatter | solution.py:34
  126.5 23.1 %collective-permute-done = f32[512,512]{0,1:T(8,128)S(1)} collective-permute-done((f32[512,512]{0,1:T(8,128)S(1)}, f32[512,512]{0,1:T(8,128)S(1)}, u32[]{:S(2)}, u32[]{:S(2)}) %collective-permute-start) | collective-permute-done | bytes 1048608 | tf_op jit(solution)/shard_map/ppermute | solution.py:16
  153.1 44.7 %collective-permute-done.1 = f32[512,512]{0,1:T(8,128)S(1)} collective-permute-done((f32[512,512]{0,1:T(8,128)S(1)}, f32[512,512]{0,1:T(8,128)S(1)}, u32[]{:S(2)}, u32[]{:S(2)}) %collective-permute-start.1) | collective-permute-done | bytes 1048608 | tf_op jit(solution)/shard_map/ppermute | solution.py:16
  202.5 23.7 %collective-permute-done.3 = f32[512,512]{0,1:T(8,128)S(1)} collective-permute-done((f32[512,512]{0,1:T(8,128)S(1)}, f32[512,512]{0,1:T(8,128)S(1)}, u32[]{:S(2)}, u32[]{:S(2)}) %collective-permute-start.3) | collective-permute-done | bytes 1048608 | tf_op jit(solution)/shard_map/ppermute | solution.py:16
  228.0 23.0 %collective-permute-done.4 = f32[512,512]{0,1:T(8,128)} collective-permute-done((f32[512,512]{0,1:T(8,128)S(1)}, f32[512,512]{0,1:T(8,128)}, u32[]{:S(2)}, u32[]{:S(2)}) %collective-permute-start.4) | collective-permute-done | bytes 1048608 | tf_op jit(solution)/shard_map/ppermute | solution.py:16
  278.2 12.1 cholesky.305
  326.8 11.9 cholesky.343
  350.5 39.3 %custom-call.30 = f32[4,128,128]{1,2,0:T(8,128)S(1)} custom-call(f32[4,128,128]{2,1,0:T(8,128)S(1)} %get-tuple-element.129), custom_call_target="InvertDiagBlocksLowerTriangular" | custom-call | tf_op jit(solution)/shard_map/triangular_solve/custom-call.3 | solution.py:45
  395.5 45.8 %all-gather.4.cloned.1.call-done = bf16[2048,512]{0,1:T(8,128)(2,1)} async-done(((bf16[512,512]{0,1:T(8,128)(2,1)}), bf16[2048,512]{0,1:T(8,128)(2,1)}) %all-gather.4.cloned.1.call-update) | async-done | bytes 2097168 | tf_op jit(solution)/shard_map/all_gather | solution.py:52
  446.8 221.1 %while.17 = (s32[]{:T(128)}, f32[16,128,512]{2,1,0:T(8,128)}, s32[16,16]{1,0:T(8,128)}, bf16[16,16,128,128]{3,2,1,0:T(8,128)(2,1)}, bf16[16,128,512]{2,1,0:T(8,128)(2,1)S(1)}, /*index=5*/f32[16,16]{1,0:T(8,128)S(1)}, s32[]{:T(128)}) while((s32[]{:T(128)}, f32[16,128,512]{2,1,0:T(8,128)}, s32[16,16]{1,0:T(8,128)}, ...), condition=%wide.region_11.15_spmd, body=%wide.region_9.14_spmd.sunk | while | flops 270532672 | bytes 17434516 | solution.py:63
  668.0 161.0 %all-gather.6.cloned.1.call-done = f32[128,128,512]{2,1,0:T(8,128)} async-done(((f32[16,128,512]{2,1,0:T(8,128)}), f32[128,128,512]{2,1,0:T(8,128)}) %all-gather.6.cloned.1.call-update) | async-done | bytes 33554448 | tf_op jit(solution)/shard_map/all_gather | solution.py:8
  828.9 13.3 %reduce_sum.9 = bf16[16,128,512]{2,1,0:T(8,128)(2,1)S(1)} reduce(f32[8,16,128,512]{3,2,1,0:T(8,128)} %bitcast.153, f32[]{:T(128)} %constant.143.clone.1), dimensions={0}, to_apply=%region_12.16 | reduce | flops 7340032 | bytes 35651588 | tf_op jit(solution)/shard_map/reduce_sum | solution.py:9
  842.2 13.8 %gather_fusion.1 = bf16[256,128,512]{2,1,0:T(8,128)(2,1)} fusion(bf16[16,128,512]{2,1,0:T(8,128)(2,1)S(1)} %reduce_sum.9, s32[1024]{0:T(1024)S(1)} %pad_clamp_fusion), kind=kCustom, calls=%fused_computation.1.clone | custom fusion | bytes 67109888 | tf_op jit(solution)/shard_map/jit(_take)/gather | solution.py:30
  856.0 19.4 %fusion.8 = f32[16,512,128,1]{1,2,3,0:T(8,128)} fusion(bf16[16,16,128,128]{3,2,1,0:T(8,128)(2,1)} %get-tuple-element.391, bf16[16,16,128,512]{3,2,1,0:T(8,128)(2,1)} %bitcast.154, pred[16,16]{1,0:T(8,128)(4,1)S(1)} %get-tuple-element.207, bf16[16,16]{1,0:T(8,128)(2,1)S(1)} %get-tuple-element.202), kind=kOutput, calls=%fused_computation.20 | convolution fusion | flops 4378853376 | bytes 46138112 | tf_op jit(solution)/shard_map/rsab,rsbk->rak/dot_general | solution.py:31
  875.5 77.0 %reduce-scatter.5.cloned.1.call-done = f32[512,512]{1,0:T(8,128)} async-done(((f32[2048,512]{1,0:T(8,128)}), f32[512,512]{1,0:T(8,128)}) %reduce-scatter.5.cloned.1.call-update) | async-done | bytes 1048592 | tf_op jit(solution)/shard_map/reduce_scatter | solution.py:34
  957.5 23.1 %collective-permute-done.5 = f32[512,512]{0,1:T(8,128)S(1)} collective-permute-done((f32[512,512]{0,1:T(8,128)S(1)}, f32[512,512]{0,1:T(8,128)S(1)}, u32[]{:S(2)}, u32[]{:S(2)}) %collective-permute-start.5) | collective-permute-done | bytes 1048608 | tf_op jit(solution)/shard_map/ppermute | solution.py:16
  984.0 44.7 %collective-permute-done.6 = f32[512,512]{0,1:T(8,128)S(1)} collective-permute-done((f32[512,512]{0,1:T(8,128)S(1)}, f32[512,512]{0,1:T(8,128)S(1)}, u32[]{:S(2)}, u32[]{:S(2)}) %collective-permute-start.6) | collective-permute-done | bytes 1048608 | tf_op jit(solution)/shard_map/ppermute | solution.py:16
  1033.4 23.7 %collective-permute-done.8 = f32[512,512]{0,1:T(8,128)S(1)} collective-permute-done((f32[512,512]{0,1:T(8,128)S(1)}, f32[512,512]{0,1:T(8,128)S(1)}, u32[]{:S(2)}, u32[]{:S(2)}) %collective-permute-start.8) | collective-permute-done | bytes 1048608 | tf_op jit(solution)/shard_map/ppermute | solution.py:16
  1058.9 22.9 %collective-permute-done.9 = f32[512,512]{0,1:T(8,128)S(1)} collective-permute-done((f32[512,512]{0,1:T(8,128)S(1)}, f32[512,512]{0,1:T(8,128)S(1)}, u32[]{:S(2)}, u32[]{:S(2)}) %collective-permute-start.9) | collective-permute-done | bytes 1048608 | tf_op jit(solution)/shard_map/ppermute | solution.py:16
  1109.4 11.9 cholesky.377
  1160.5 11.9 cholesky.415
  1191.3 40.1 %custom-call.34 = f32[4,128,128]{1,2,0:T(8,128)S(1)} custom-call(f32[4,128,128]{2,1,0:T(8,128)} %copy-done.6), custom_call_target="InvertDiagBlocksLowerTriangular" | custom-call | tf_op jit(solution)/shard_map/triangular_solve/custom-call.3 | solution.py:45
  (216 shorter events, 450.9 us)
Async XLA Ops:
  7.2 1.8 copy-start
  7.2 114.4 %reduce-scatter.3.cloned.1.call-start = ((), (), s32[]{:S(2)}) async-start(), calls=%async_computation.2 | async-start | bytes 5242880 | tf_op jit(solution)/shard_map/reduce_scatter | solution.py:34
  41.9 399.5 %all-gather.4.cloned.1.call-start = ((), (), s32[]{:S(2)}) async-start(), calls=%async_computation.3 | async-start | bytes 2621440 | tf_op jit(solution)/shard_map/all_gather | solution.py:52
  125.0 24.7 %collective-permute-start = (f32[512,512]{0,1:T(8,128)S(1)}, f32[512,512]{0,1:T(8,128)S(1)}, u32[]{:S(2)}, u32[]{:S(2)}) collective-permute-start(f32[512,512]{0,1:T(8,128)S(1)} %fusion.93), channel_id=1, source_target_pairs={{0,1},{1,0},{2,3},{3,2},{4,5},{5,4},{6,7},{7,6},{8,9},{9,8},{10,11... | collective-permute-start | bytes 3145736 | tf_op jit(solution)/shard_map/ppermute | solution.py:16
  149.9 48.0 %collective-permute-start.1 = (f32[512,512]{0,1:T(8,128)S(1)}, f32[512,512]{0,1:T(8,128)S(1)}, u32[]{:S(2)}, u32[]{:S(2)}) collective-permute-start(f32[512,512]{0,1:T(8,128)S(1)} %add.111), channel_id=1, source_target_pairs={{0,2},{1,3},{2,0},{3,1},{4,6},{5,7},{6,4},{7,5},{8,10},{9,11},{10,... | collective-permute-start | bytes 3145736 | tf_op jit(solution)/shard_map/ppermute | solution.py:16
  198.0 2.7 collective-permute-start.2
  201.0 25.3 %collective-permute-start.3 = (f32[512,512]{0,1:T(8,128)S(1)}, f32[512,512]{0,1:T(8,128)S(1)}, u32[]{:S(2)}, u32[]{:S(2)}) collective-permute-start(f32[512,512]{0,1:T(8,128)S(1)} %add.113), channel_id=1, source_target_pairs={{0,8},{1,9},{2,10},{3,11},{4,12},{5,13},{6,14},{7,15},{8,0},{9,1},... | collective-permute-start | bytes 3145736 | tf_op jit(solution)/shard_map/ppermute | solution.py:16
  226.5 163.4 %copy-start.2 = (f32[512,512]{1,0:T(8,128)S(1)}, f32[512,512]{1,0:T(8,128)}, u32[]{:S(2)}) copy-start(f32[512,512]{1,0:T(8,128)} %reduce-scatter.3.cloned.1.call-done) | copy-start | bytes 3145732
  226.5 24.5 %collective-permute-start.4 = (f32[512,512]{0,1:T(8,128)S(1)}, f32[512,512]{0,1:T(8,128)}, u32[]{:S(2)}, u32[]{:S(2)}) collective-permute-start(f32[512,512]{0,1:T(8,128)S(1)} %add.114), channel_id=1, source_target_pairs={{0,16},{1,17},{2,18},{3,19},{4,20},{5,21},{6,22},{7,23},{8,24},{9,... | collective-permute-start | bytes 3145736 | tf_op jit(solution)/shard_map/ppermute | solution.py:16
  253.0 1.0 copy-start.4
  395.5 433.4 %all-gather.6.cloned.1.call-start = ((), (), s32[]{:S(2)}) async-start(), calls=%async_computation.5 | async-start | bytes 37748736 | tf_op jit(solution)/shard_map/all_gather | solution.py:8
  667.9 284.6 %reduce-scatter.5.cloned.1.call-start = ((), (), s32[]{:S(2)}) async-start(), calls=%async_computation.4 | async-start | bytes 5242880 | tf_op jit(solution)/shard_map/reduce_scatter | solution.py:34
  955.9 24.7 %collective-permute-start.5 = (f32[512,512]{0,1:T(8,128)S(1)}, f32[512,512]{0,1:T(8,128)S(1)}, u32[]{:S(2)}, u32[]{:S(2)}) collective-permute-start(f32[512,512]{0,1:T(8,128)S(1)} %fusion.94), channel_id=1, source_target_pairs={{0,1},{1,0},{2,3},{3,2},{4,5},{5,4},{6,7},{7,6},{8,9},{9,8},{10,11... | collective-permute-start | bytes 3145736 | tf_op jit(solution)/shard_map/ppermute | solution.py:16
  980.8 47.9 %collective-permute-start.6 = (f32[512,512]{0,1:T(8,128)S(1)}, f32[512,512]{0,1:T(8,128)S(1)}, u32[]{:S(2)}, u32[]{:S(2)}) collective-permute-start(f32[512,512]{0,1:T(8,128)S(1)} %add.116), channel_id=1, source_target_pairs={{0,2},{1,3},{2,0},{3,1},{4,6},{5,7},{6,4},{7,5},{8,10},{9,11},{10,... | collective-permute-start | bytes 3145736 | tf_op jit(solution)/shard_map/ppermute | solution.py:16
  1028.9 2.7 collective-permute-start.7
  1031.9 25.3 %collective-permute-start.8 = (f32[512,512]{0,1:T(8,128)S(1)}, f32[512,512]{0,1:T(8,128)S(1)}, u32[]{:S(2)}, u32[]{:S(2)}) collective-permute-start(f32[512,512]{0,1:T(8,128)S(1)} %add.118), channel_id=1, source_target_pairs={{0,8},{1,9},{2,10},{3,11},{4,12},{5,13},{6,14},{7,15},{8,0},{9,1},... | collective-permute-start | bytes 3145736 | tf_op jit(solution)/shard_map/ppermute | solution.py:16
  1057.3 174.0 %copy-start.3 = (f32[512,512]{1,0:T(8,128)S(1)}, f32[512,512]{1,0:T(8,128)}, u32[]{:S(2)}) copy-start(f32[512,512]{1,0:T(8,128)} %reduce-scatter.5.cloned.1.call-done) | copy-start | bytes 3145732
  1057.4 24.4 %collective-permute-start.9 = (f32[512,512]{0,1:T(8,128)S(1)}, f32[512,512]{0,1:T(8,128)S(1)}, u32[]{:S(2)}, u32[]{:S(2)}) collective-permute-start(f32[512,512]{0,1:T(8,128)S(1)} %add.119), channel_id=1, source_target_pairs={{0,16},{1,17},{2,18},{3,19},{4,20},{5,21},{6,22},{7,23},{8,24},{9,... | collective-permute-start | bytes 3145736 | tf_op jit(solution)/shard_map/ppermute | solution.py:16
  1082.6 1.0 copy-start.5
  1158.3 84.5 %copy-start.1 = (bf16[2048,512]{1,0:T(8,128)(2,1)S(1)}, bf16[2048,512]{1,0:T(8,128)(2,1)}, u32[]{:S(2)}) copy-start(bf16[2048,512]{1,0:T(8,128)(2,1)} %param.14) | copy-start | bytes 6291460
  1190.6 0.7 copy-start.6
Sparse Core Ops, SparseCore 0:
  42.0 79.5 reduce-scatter.2
  395.6 45.7 all-gather.3
  668.1 160.8 all-gather.5
  875.6 76.8 reduce-scatter.4
